TPU v7x, 32 devices: a whole 2x2x4 slice. The times are simulated.
32 devices in a mesh: band: 2 (over y), row: 16 (over z, x, core).
Axes of the slice: x: 2, y: 2, z: 4, core: 2. Of those that a mesh axis runs over, the one named last changes fastest.
Arguments:
- coeffs: bfloat16 [2, 6144, 4096], P(None, 'row', 'band'), may hold values from -6 to 6
- rotation: bfloat16 [2, 4096, 4096], P(None, 'row', 'band'), may hold values from -0.0625 to 0.0625
Outputs:
- rotated: bfloat16 [2, 6144, 4096], P(None, 'row', 'band')
All inputs are finite; a program needn't handle non-finite values.
Results may differ from a plain program's by a relative error of at most 0.0014.
Values may be sent and summed in bfloat16 or wider, within the bound.
A program may use at most 128 MiB of HBM per device.

v0:
```python
import jax
import jax.numpy as jnp
from jax import lax
from jax.sharding import PartitionSpec as P


def complex_product(left, right):
    real_out = jnp.dot(left[0], right[0], preferred_element_type=jnp.float32) - jnp.dot(
        left[1], right[1], preferred_element_type=jnp.float32
    )
    imag_out = jnp.dot(left[0], right[1], preferred_element_type=jnp.float32) + jnp.dot(
        left[1], right[0], preferred_element_type=jnp.float32
    )
    return jnp.stack([real_out, imag_out])


def body(coeffs, rotation):
    whole_coeffs = lax.all_gather(coeffs, "band", axis=2, tiled=True)
    summed = complex_product(whole_coeffs, lax.all_gather(rotation, "row", axis=1, tiled=True))
    return summed.astype(jnp.bfloat16)


def solution(mesh):
    in_specs = (P(None, "row", "band"), P(None, "row", "band"))
    out_specs = P(None, "row", "band")
    return jax.shard_map(body, mesh=mesh, in_specs=in_specs, out_specs=out_specs, check_vma=False)
```

profile of v0, /device:TPU:0, one launch (start us, length us, event | category | flops | bytes accessed | tf_op | source)
XLA Modules:
  0.0 312.7 jit_solution(16313356740917416419)
XLA Ops:
  6.5 0.0 all-gather.3.cloned.1.call-start
  6.5 0.7 all-gather.3.cloned.1.call-update
  7.3 0.0 all-gather.5.cloned.1.call-start
  7.3 0.7 all-gather.5.cloned.1.call-update
  8.0 84.0 %all-gather.3.cloned.1.call-done = bf16[2,384,4096]{2,1,0:T(8,128)(2,1)} async-done(((bf16[2,384,2048]{2,1,0:T(8,128)(2,1)}), bf16[2,384,4096]{2,1,0:T(8,128)(2,1)}) %all-gather.3.cloned.1.call-update) | async-done | bytes 6291472 | tf_op jit(solution)/shard_map/all_gather | solution.py:18
  92.0 169.6 %all-gather.5.cloned.1.call-done = bf16[2,4096,2048]{2,1,0:T(8,128)(2,1)} async-done(((bf16[2,256,2048]{2,1,0:T(8,128)(2,1)}), bf16[2,4096,2048]{2,1,0:T(8,128)(2,1)}) %all-gather.5.cloned.1.call-update) | async-done | bytes 33554448 | tf_op jit(solution)/shard_map/all_gather | solution.py:19
  261.6 0.0 copy-start
  261.6 11.3 %fusion = f32[384,2048]{1,0:T(8,128)S(1)} fusion(bf16[2,4096,2048]{2,1,0:T(8,128)(2,1)} %all-gather.5.cloned.1.call-done, bf16[2,384,4096]{2,1,0:T(8,128)(2,1)} %all-gather.3.cloned.1.call-done), kind=kOutput, calls=%fused_computation.2 | convolution fusion | flops 6442450944 | bytes 23068672 | tf_op jit(solution)/shard_map/dot_general | solution.py:11
  272.9 0.0 copy-done
  272.9 10.3 %fusion.1 = f32[384,2048]{1,0:T(8,128)S(1)} fusion(bf16[2,4096,2048]{2,1,0:T(8,128)(2,1)} %all-gather.5.cloned.1.call-done, bf16[2,384,4096]{2,1,0:T(8,128)(2,1)S(1)} %copy-done), kind=kOutput, calls=%fused_computation.3 | convolution fusion | flops 6442450944 | bytes 23068672 | tf_op jit(solution)/shard_map/dot_general | solution.py:8
  283.2 10.4 %fusion.5 = bf16[1,384,2048]{2,1,0:T(8,128)(2,1)S(1)} fusion(f32[384,2048]{1,0:T(8,128)S(1)} %fusion, bf16[2,4096,2048]{2,1,0:T(8,128)(2,1)} %all-gather.5.cloned.1.call-done, bf16[2,384,4096]{2,1,0:T(8,128)(2,1)S(1)} %copy-done), kind=kOutput, calls=%fused_computation.12 | convolution fusion | flops 6444023808 | bytes 24641536 | tf_op jit(solution)/shard_map/dot_general | solution.py:11
  293.6 10.4 %fusion.4 = bf16[1,384,2048]{2,1,0:T(8,128)(2,1)S(1)} fusion(f32[384,2048]{1,0:T(8,128)S(1)} %fusion.1, bf16[2,4096,2048]{2,1,0:T(8,128)(2,1)} %all-gather.5.cloned.1.call-done, bf16[2,384,4096]{2,1,0:T(8,128)(2,1)S(1)} %copy-done), kind=kOutput, calls=%fused_computation.11 | convolution fusion | flops 6444023808 | bytes 24641536 | tf_op jit(solution)/shard_map/dot_general | solution.py:8
  303.9 1.9 pad_maximum_fusion
Async XLA Ops:
  6.5 85.5 %all-gather.3.cloned.1.call-start = ((), (), s32[]{:S(2)}) async-start(), calls=%async_computation | async-start | bytes 9437184 | tf_op jit(solution)/shard_map/all_gather | solution.py:18
  7.3 254.4 %all-gather.5.cloned.1.call-start = ((), (), s32[]{:S(2)}) async-start(), calls=%async_computation.1 | async-start | bytes 35651584 | tf_op jit(solution)/shard_map/all_gather | solution.py:19
  261.6 11.3 %copy-start = (bf16[2,384,4096]{2,1,0:T(8,128)(2,1)S(1)}, bf16[2,384,4096]{2,1,0:T(8,128)(2,1)}, u32[]{:S(2)}) copy-start(bf16[2,384,4096]{2,1,0:T(8,128)(2,1)} %all-gather.3.cloned.1.call-done) | copy-start | bytes 18874372
Sparse Core Ops, SparseCore 0:
  8.9 83.0 all-gather.2
  93.5 168.0 all-gather.4
where the time goes:
time: 313 us
  waiting for transfers between devices  255 us (81%)
  matrix products  42.3 us (14%)
  between operations  13.4 us (4%)
    all_gather x1, waiting for transfers between devices, body(): lax.all_gather(rotation, 'row', axis=1, tiled=True)  170 us
    all_gather x1, waiting for transfers between devices, body(): whole_coeffs = lax.all_gather(coeffs, 'band', axis=2, tiled=True)  84 us
    dot_general x1, matrix products, complex_product(): jnp.dot(left[1], right[0], preferred_element_type=jnp.float32)  11.3 us
    dot_general x1, matrix products, complex_product(): jnp.dot(left[0], right[1], preferred_element_type=jnp.float32)  10.4 us
    dot_general x1, matrix products, complex_product(): jnp.dot(left[1], right[1], preferred_element_type=jnp.float32)  10.4 us
    dot_general x1, matrix products, complex_product(): jnp.dot(left[0], right[0], preferred_element_type=jnp.float32)  10.3 us
  transfers between devices with their start and end apart: 2, of which 2 were waited for; matrix products, arithmetic and copies ran while one was open for 0% of the time, Pallas kernels for 0%

commit v1 on v0

v1 whole, which is shorter than its diff:
```python
import jax
import jax.numpy as jnp
from jax import lax
from jax.sharding import PartitionSpec as P

CHUNKS = 4


def complex_product(left, right):
    real_out = jnp.dot(left[0], right[0], preferred_element_type=jnp.float32) - jnp.dot(
        left[1], right[1], preferred_element_type=jnp.float32
    )
    imag_out = jnp.dot(left[0], right[1], preferred_element_type=jnp.float32) + jnp.dot(
        left[1], right[0], preferred_element_type=jnp.float32
    )
    return jnp.stack([real_out, imag_out])


def solution(mesh):
    bands = mesh.shape["band"]

    def body(coeffs, rotation):
        me = lax.axis_index("band")
        width = coeffs.shape[2]
        whole = jnp.zeros(coeffs.shape[:2] + (width * bands,), coeffs.dtype)
        whole = lax.dynamic_update_slice_in_dim(whole, coeffs, me * width, 2)
        for step in range(1, bands):
            perm = [(i, (i + step) % bands) for i in range(bands)]
            block = lax.ppermute(coeffs, "band", perm)
            owner = lax.rem(me - step + bands, bands)
            whole = lax.dynamic_update_slice_in_dim(whole, block, owner * width, 2)
        columns = rotation.shape[2] // CHUNKS
        outs = []
        for chunk in range(CHUNKS):
            piece = rotation[:, :, chunk * columns : (chunk + 1) * columns]
            gathered = lax.all_gather(piece, "row", axis=1, tiled=True)
            outs.append(complex_product(whole, gathered).astype(jnp.bfloat16))
        return jnp.concatenate(outs, axis=2)

    in_specs = (P(None, "row", "band"), P(None, "row", "band"))
    out_specs = P(None, "row", "band")
    return jax.shard_map(body, mesh=mesh, in_specs=in_specs, out_specs=out_specs, check_vma=False)
```

time: 313 us -> 361 us (1.15)
  matrix products: 42.3 us -> 68.2 us
  local copies, waits for them, and re-layouts: 0.01 us -> 13.3 us
  waiting for transfers between devices: 255 us -> 260 us
    ppermute x0 -> x1, waiting for transfers between devices: none -> 62.8 us  [body(): block = lax.ppermute(coeffs, 'band', perm)]
    all_gather x2 -> x4, waiting for transfers between devices: 254 us -> 196 us  [body(): gathered = lax.all_gather(piece, 'row', axis=1, tiled=True)]
    dot_general x1 -> x4, matrix products: 10.4 us -> 22 us  [complex_product(): jnp.dot(left[1], right[1], preferred_element_type=jnp.float32)]
    dynamic_update_slice x0 -> x2, local copies, waits for them, and re-layouts: none -> 5.95 us  [the longest x1 3.91 us: body(): whole = lax.dynamic_update_slice_in_dim(whole, block, owner * width, 2)]
    dot_general x1 -> x4, matrix products: 10.3 us -> 15.2 us  [complex_product(): jnp.dot(left[0], right[0], preferred_element_type=jnp.float32)]
    dot_general x1 -> x4, matrix products: 11.3 us -> 16 us  [complex_product(): jnp.dot(left[1], right[0], preferred_element_type=jnp.float32)]
    dot_general x1 -> x4, matrix products: 10.4 us -> 15 us  [complex_product(): jnp.dot(left[0], right[1], preferred_element_type=jnp.float32)]
  transfers between devices with their start and end apart: 2 -> 5, of which waited for: 2 -> 4; matrix products, arithmetic and copies ran while one was open for 0% -> 11% of each run, Pallas kernels for 0% -> 0%
where the time goes in v1:
time: 361 us; the launch traced here: 360 us
  waiting for transfers between devices  260 us (72%)
  matrix products  68.2 us (19%)
  between operations  13.4 us (4%)
  local copies, waits for them, and re-layouts  13.3 us (4%)
    all_gather x4, waiting for transfers between devices, body(): gathered = lax.all_gather(piece, 'row', axis=1, tiled=True)  196 us
    ppermute x1, waiting for transfers between devices, body(): block = lax.ppermute(coeffs, 'band', perm)  62.8 us
    dot_general x4, matrix products, complex_product(): jnp.dot(left[1], right[1], preferred_element_type=jnp.float32)  22 us
    dot_general x4, matrix products, complex_product(): jnp.dot(left[1], right[0], preferred_element_type=jnp.float32)  16 us
    dot_general x4, matrix products, complex_product(): jnp.dot(left[0], right[0], preferred_element_type=jnp.float32)  15.2 us
    dot_general x4, matrix products, complex_product(): jnp.dot(left[0], right[1], preferred_element_type=jnp.float32)  15 us
  transfers between devices with their start and end apart: 5, of which 4 were waited for; matrix products, arithmetic and copies ran while one was open for 11% of the time, Pallas kernels for 0%

profile of v1, /device:TPU:0, one launch (start us, length us, event | category | flops | bytes accessed | tf_op | source)
XLA Modules:
  0.0 360.3 jit_solution(15331581861062025627)
XLA Ops:
  6.5 0.0 copy-start
  6.5 0.0 all-gather.5.cloned.1.call-start
  6.5 3.0 fusion.40
  9.6 0.0 all-gather.5.cloned.1.call-update
  9.6 0.0 all-gather.7.cloned.1.call-start
  9.6 0.7 all-gather.7.cloned.1.call-update
  10.3 0.0 all-gather.9.cloned.1.call-start
  10.4 0.7 all-gather.9.cloned.1.call-update
  11.1 0.0 all-gather.11.cloned.1.call-start
  11.1 0.5 all-gather.11.cloned.1.call-update
  11.7 0.0 copy-done
  11.7 3.1 collective-permute-start
  14.7 3.4 broadcast_in_dim.3
  18.1 2.0 constant_dynamic-update-slice_fusion.1
  20.1 62.8 %collective-permute-done = bf16[2,384,2048]{2,1,0:T(8,128)(2,1)} collective-permute-done((bf16[2,384,2048]{2,1,0:T(8,128)(2,1)S(1)}, bf16[2,384,2048]{2,1,0:T(8,128)(2,1)}, u32[]{:S(2)}, u32[]{:S(2)}) %collective-permute-start) | collective-permute-done | bytes 3145760 | tf_op jit(solution)/shard_map/ppermute | solution.py:29
  82.9 3.9 %constant_dynamic-update-slice_fusion = bf16[2,384,4096]{2,1,0:T(8,128)(2,1)} fusion(bf16[2,384,4096]{2,1,0:T(8,128)(2,1)} %constant_dynamic-update-slice_fusion.1, bf16[2,384,2048]{2,1,0:T(8,128)(2,1)} %collective-permute-done, s32[]{:T(128)S(6)} %select_n.7), kind=kLoop, calls=%fused_computation.51 | loop fusion | bytes 6291460 | tf_op jit(solution)/shard_map/dynamic_update_slice | solution.py:31
  86.8 0.0 all-gather.5.cloned.1.call-done
  86.8 0.0 copy-start.1
  86.9 5.1 %fusion.3 = f32[384,512]{1,0:T(8,128)S(1)} fusion(bf16[2,4096,512]{2,1,0:T(8,128)(2,1)} %all-gather.5.cloned.1.call-done, bf16[2,384,4096]{2,1,0:T(8,128)(2,1)} %constant_dynamic-update-slice_fusion), kind=kOutput, calls=%fused_computation.11 | convolution fusion | flops 1610612736 | bytes 8126464 | tf_op jit(solution)/shard_map/dot_general | solution.py:10
  91.9 0.5 copy-done.1
  92.4 3.7 %fusion = f32[384,512]{1,0:T(8,128)S(1)} fusion(bf16[2,4096,512]{2,1,0:T(8,128)(2,1)S(1)} %copy-done.1, bf16[2,384,4096]{2,1,0:T(8,128)(2,1)} %constant_dynamic-update-slice_fusion), kind=kOutput, calls=%fused_computation.8 | convolution fusion | flops 1610612736 | bytes 8126464 | tf_op jit(solution)/shard_map/dot_general | solution.py:13
  96.1 65.8 %all-gather.7.cloned.1.call-done = bf16[2,4096,512]{2,1,0:T(8,128)(2,1)} async-done(((bf16[2,256,512]{2,1,0:T(8,128)(2,1)}), bf16[2,4096,512]{2,1,0:T(8,128)(2,1)}) %all-gather.7.cloned.1.call-update) | async-done | bytes 8388624 | tf_op jit(solution)/shard_map/all_gather | solution.py:36
  161.9 0.0 copy-start.2
  161.9 6.0 %fusion.7 = f32[384,512]{1,0:T(8,128)} fusion(bf16[2,4096,512]{2,1,0:T(8,128)(2,1)} %all-gather.7.cloned.1.call-done, bf16[2,384,4096]{2,1,0:T(8,128)(2,1)} %constant_dynamic-update-slice_fusion), kind=kOutput, calls=%fused_computation.15 | convolution fusion | flops 1610612736 | bytes 8126464 | tf_op jit(solution)/shard_map/dot_general | solution.py:10
  167.9 0.0 copy-done.2
  167.9 3.7 %fusion.4 = f32[384,512]{1,0:T(8,128)S(1)} fusion(bf16[2,4096,512]{2,1,0:T(8,128)(2,1)S(1)} %copy-done.2, bf16[2,384,4096]{2,1,0:T(8,128)(2,1)} %constant_dynamic-update-slice_fusion), kind=kOutput, calls=%fused_computation.12 | convolution fusion | flops 1610612736 | bytes 8126464 | tf_op jit(solution)/shard_map/dot_general | solution.py:13
  171.6 65.4 %all-gather.9.cloned.1.call-done = bf16[2,4096,512]{2,1,0:T(8,128)(2,1)} async-done(((bf16[2,256,512]{2,1,0:T(8,128)(2,1)}), bf16[2,4096,512]{2,1,0:T(8,128)(2,1)}) %all-gather.9.cloned.1.call-update) | async-done | bytes 8388624 | tf_op jit(solution)/shard_map/all_gather | solution.py:36
  237.0 0.0 copy-start.3
  237.0 6.0 %fusion.11 = f32[384,512]{1,0:T(8,128)} fusion(bf16[2,4096,512]{2,1,0:T(8,128)(2,1)} %all-gather.9.cloned.1.call-done, bf16[2,384,4096]{2,1,0:T(8,128)(2,1)} %constant_dynamic-update-slice_fusion), kind=kOutput, calls=%fused_computation.19 | convolution fusion | flops 1610612736 | bytes 8126464 | tf_op jit(solution)/shard_map/dot_general | solution.py:10
  243.0 0.0 copy-done.3
  243.0 4.7 %fusion.8 = f32[384,512]{1,0:T(8,128)} fusion(bf16[2,4096,512]{2,1,0:T(8,128)(2,1)S(1)} %copy-done.3, bf16[2,384,4096]{2,1,0:T(8,128)(2,1)} %constant_dynamic-update-slice_fusion), kind=kOutput, calls=%fused_computation.16 | convolution fusion | flops 1610612736 | bytes 8126464 | tf_op jit(solution)/shard_map/dot_general | solution.py:13
  247.6 64.4 %all-gather.11.cloned.1.call-done = bf16[2,4096,512]{2,1,0:T(8,128)(2,1)} async-done(((bf16[2,256,512]{2,1,0:T(8,128)(2,1)}), bf16[2,4096,512]{2,1,0:T(8,128)(2,1)}) %all-gather.11.cloned.1.call-update) | async-done | bytes 8388624 | tf_op jit(solution)/shard_map/all_gather | solution.py:36
  312.0 0.0 copy-start.4
  312.0 0.0 slice-start
  312.0 5.1 %fusion.15 = f32[384,512]{1,0:T(8,128)S(1)} fusion(bf16[2,4096,512]{2,1,0:T(8,128)(2,1)} %all-gather.11.cloned.1.call-done, bf16[2,384,4096]{2,1,0:T(8,128)(2,1)} %constant_dynamic-update-slice_fusion), kind=kOutput, calls=%fused_computation.23 | convolution fusion | flops 1610612736 | bytes 8126464 | tf_op jit(solution)/shard_map/dot_general | solution.py:10
  317.0 0.5 copy-done.4
  317.5 0.0 slice-start.1
  317.5 3.9 %fusion.12 = f32[384,512]{1,0:T(8,128)S(1)} fusion(bf16[2,4096,512]{2,1,0:T(8,128)(2,1)S(1)} %copy-done.4, bf16[2,384,4096]{2,1,0:T(8,128)(2,1)} %constant_dynamic-update-slice_fusion), kind=kOutput, calls=%fused_computation.20 | convolution fusion | flops 1610612736 | bytes 8126464 | tf_op jit(solution)/shard_map/dot_general | solution.py:13
  321.4 0.0 slice-done
  321.4 0.0 slice-done.1
  321.4 0.0 slice-start.2
  321.4 3.8 %fusion.39 = bf16[1,384,512]{2,1,0:T(8,128)(2,1)S(1)} fusion(f32[384,512]{1,0:T(8,128)S(1)} %fusion.3, bf16[2,4096,512]{2,1,0:T(8,128)(2,1)S(1)} %bitcast.117, bf16[2,384,4096]{2,1,0:T(8,128)(2,1)} %constant_dynamic-update-slice_fusion), kind=kOutput, calls=%fused_computation.50 | convolution fusion | flops 1611005952 | bytes 8519680 | tf_op jit(solution)/shard_map/dot_general | solution.py:10
  325.2 0.0 slice-start.3
  325.2 0.0 copy-start.6
  325.3 3.8 %fusion.38 = bf16[1,384,512]{2,1,0:T(8,128)(2,1)S(1)} fusion(f32[384,512]{1,0:T(8,128)S(1)} %fusion, bf16[2,4096,512]{2,1,0:T(8,128)(2,1)S(1)} %bitcast.117, bf16[2,384,4096]{2,1,0:T(8,128)(2,1)} %constant_dynamic-update-slice_fusion), kind=kOutput, calls=%fused_computation.49 | convolution fusion | flops 1611005952 | bytes 8519680 | tf_op jit(solution)/shard_map/dot_general | solution.py:13
  329.1 0.0 slice-done.2
  329.1 0.0 slice-done.3
  329.1 0.0 copy-done.6
  329.1 0.0 slice-start.4
  329.1 4.0 %fusion.37 = bf16[1,384,512]{2,1,0:T(8,128)(2,1)S(1)} fusion(f32[384,512]{1,0:T(8,128)S(1)} %copy-done.6, bf16[2,4096,512]{2,1,0:T(8,128)(2,1)S(1)} %bitcast.119, bf16[2,384,4096]{2,1,0:T(8,128)(2,1)} %constant_dynamic-update-slice_fusion), kind=kOutput, calls=%fused_computation.48 | convolution fusion | flops 1611005952 | bytes 8519680 | tf_op jit(solution)/shard_map/dot_general | solution.py:10
  333.1 0.0 slice-start.5
  333.1 0.0 copy-start.7
  333.2 3.8 %fusion.36 = bf16[1,384,512]{2,1,0:T(8,128)(2,1)S(1)} fusion(f32[384,512]{1,0:T(8,128)S(1)} %fusion.4, bf16[2,4096,512]{2,1,0:T(8,128)(2,1)S(1)} %bitcast.119, bf16[2,384,4096]{2,1,0:T(8,128)(2,1)} %constant_dynamic-update-slice_fusion), kind=kOutput, calls=%fused_computation.47 | convolution fusion | flops 1611005952 | bytes 8519680 | tf_op jit(solution)/shard_map/dot_general | solution.py:13
  337.0 0.0 slice-done.4
  337.0 0.0 slice-done.5
  337.0 0.0 copy-done.7
  337.0 0.0 copy-start.5
  337.0 3.7 %fusion.35 = bf16[1,384,512]{2,1,0:T(8,128)(2,1)S(1)} fusion(f32[384,512]{1,0:T(8,128)S(1)} %copy-done.7, bf16[2,4096,512]{2,1,0:T(8,128)(2,1)S(1)} %bitcast.121, bf16[2,384,4096]{2,1,0:T(8,128)(2,1)} %constant_dynamic-update-slice_fusion), kind=kOutput, calls=%fused_computation.46 | convolution fusion | flops 1611005952 | bytes 8519680 | tf_op jit(solution)/shard_map/dot_general | solution.py:10
  340.8 0.0 copy-done.5
  340.8 3.7 %fusion.34 = bf16[1,384,512]{2,1,0:T(8,128)(2,1)S(1)} fusion(f32[384,512]{1,0:T(8,128)S(1)} %copy-done.5, bf16[2,4096,512]{2,1,0:T(8,128)(2,1)S(1)} %bitcast.121, bf16[2,384,4096]{2,1,0:T(8,128)(2,1)} %constant_dynamic-update-slice_fusion), kind=kOutput, calls=%fused_computation.45 | convolution fusion | flops 1611005952 | bytes 8519680 | tf_op jit(solution)/shard_map/dot_general | solution.py:13
  344.5 3.7 %fusion.33 = bf16[1,384,512]{2,1,0:T(8,128)(2,1)S(1)} fusion(f32[384,512]{1,0:T(8,128)S(1)} %fusion.15, bf16[2,4096,512]{2,1,0:T(8,128)(2,1)S(1)} %copy-done.4, bf16[2,384,4096]{2,1,0:T(8,128)(2,1)} %constant_dynamic-update-slice_fusion), kind=kOutput, calls=%fused_computation.44 | convolution fusion | flops 1611005952 | bytes 8519680 | tf_op jit(solution)/shard_map/dot_general | solution.py:10
  348.1 3.7 %fusion.32 = bf16[1,384,512]{2,1,0:T(8,128)(2,1)S(1)} fusion(f32[384,512]{1,0:T(8,128)S(1)} %fusion.12, bf16[2,4096,512]{2,1,0:T(8,128)(2,1)S(1)} %copy-done.4, bf16[2,384,4096]{2,1,0:T(8,128)(2,1)} %constant_dynamic-update-slice_fusion), kind=kOutput, calls=%fused_computation.43 | convolution fusion | flops 1611005952 | bytes 8519680 | tf_op jit(solution)/shard_map/dot_general | solution.py:13
  351.8 1.9 maximum_maximum_fusion
  (3 shorter events, 0.0 us)
Async XLA Ops:
  6.5 5.1 %copy-start = (bf16[2,384,2048]{2,1,0:T(8,128)(2,1)S(1)}, bf16[2,384,2048]{2,1,0:T(8,128)(2,1)}, u32[]{:S(2)}) copy-start(bf16[2,384,2048]{2,1,0:T(8,128)(2,1)} %param.2) | copy-start | bytes 9437188
  6.5 80.3 %all-gather.5.cloned.1.call-start = ((), (), s32[]{:S(2)}) async-start(), calls=%async_computation | async-start | bytes 8912896 | tf_op jit(solution)/shard_map/all_gather | solution.py:36
  9.6 152.3 %all-gather.7.cloned.1.call-start = ((), (), s32[]{:S(2)}) async-start(), calls=%async_computation.1 | async-start | bytes 8912896 | tf_op jit(solution)/shard_map/all_gather | solution.py:36
  10.3 226.7 %all-gather.9.cloned.1.call-start = ((), (), s32[]{:S(2)}) async-start(), calls=%async_computation.2 | async-start | bytes 8912896 | tf_op jit(solution)/shard_map/all_gather | solution.py:36
  11.1 300.9 %all-gather.11.cloned.1.call-start = ((), (), s32[]{:S(2)}) async-start(), calls=%async_computation.3 | async-start | bytes 8912896 | tf_op jit(solution)/shard_map/all_gather | solution.py:36
  11.7 71.3 %collective-permute-start = (bf16[2,384,2048]{2,1,0:T(8,128)(2,1)S(1)}, bf16[2,384,2048]{2,1,0:T(8,128)(2,1)}, u32[]{:S(2)}, u32[]{:S(2)}) collective-permute-start(bf16[2,384,2048]{2,1,0:T(8,128)(2,1)S(1)} %copy-done), channel_id=1, source_target_pairs={{0,16},{16,0},{1,17},{17,1},{2,18},{18,2},{3,19},{19,3},{4,20},{20... | collective-permute-start | bytes 9437192 | tf_op jit(solution)/shard_map/ppermute | solution.py:29
  86.8 5.5 %copy-start.1 = (bf16[2,4096,512]{2,1,0:T(8,128)(2,1)S(1)}, bf16[2,4096,512]{2,1,0:T(8,128)(2,1)}, u32[]{:S(2)}) copy-start(bf16[2,4096,512]{2,1,0:T(8,128)(2,1)} %all-gather.5.cloned.1.call-done) | copy-start | bytes 25165828
  161.9 6.0 %copy-start.2 = (bf16[2,4096,512]{2,1,0:T(8,128)(2,1)S(1)}, bf16[2,4096,512]{2,1,0:T(8,128)(2,1)}, u32[]{:S(2)}) copy-start(bf16[2,4096,512]{2,1,0:T(8,128)(2,1)} %all-gather.7.cloned.1.call-done) | copy-start | bytes 25165828
  237.0 6.0 %copy-start.3 = (bf16[2,4096,512]{2,1,0:T(8,128)(2,1)S(1)}, bf16[2,4096,512]{2,1,0:T(8,128)(2,1)}, u32[]{:S(2)}) copy-start(bf16[2,4096,512]{2,1,0:T(8,128)(2,1)} %all-gather.9.cloned.1.call-done) | copy-start | bytes 25165828
  312.0 5.5 %copy-start.4 = (bf16[2,4096,512]{2,1,0:T(8,128)(2,1)S(1)}, bf16[2,4096,512]{2,1,0:T(8,128)(2,1)}, u32[]{:S(2)}) copy-start(bf16[2,4096,512]{2,1,0:T(8,128)(2,1)} %all-gather.11.cloned.1.call-done) | copy-start | bytes 25165828
  312.0 9.4 %slice-start = ((s8[8388608]{0:T(1024)(128)(4,1)}), s8[4194304]{0:T(1024)(128)(4,1)S(1)}, s32[]{:S(2)}) async-start(s8[8388608]{0:T(1024)(128)(4,1)} %bitcast.116), calls=%async_computation.4 | async-start | bytes 8388608
  317.5 3.9 %slice-start.1 = ((s8[8388608]{0:T(1024)(128)(4,1)}), s8[4194304]{0:T(1024)(128)(4,1)S(1)}, s32[]{:S(2)}) async-start(s8[8388608]{0:T(1024)(128)(4,1)} %bitcast.116), calls=%async_computation.5 | async-start | bytes 8388608
  321.4 7.7 %slice-start.2 = ((s8[8388608]{0:T(1024)(128)(4,1)}), s8[4194304]{0:T(1024)(128)(4,1)S(1)}, s32[]{:S(2)}) async-start(s8[8388608]{0:T(1024)(128)(4,1)} %bitcast.118), calls=%async_computation.6 | async-start | bytes 8388608
  325.2 3.9 %slice-start.3 = ((s8[8388608]{0:T(1024)(128)(4,1)}), s8[4194304]{0:T(1024)(128)(4,1)S(1)}, s32[]{:S(2)}) async-start(s8[8388608]{0:T(1024)(128)(4,1)} %bitcast.118), calls=%async_computation.7 | async-start | bytes 8388608
  325.2 3.9 %copy-start.6 = (f32[384,512]{1,0:T(8,128)S(1)}, f32[384,512]{1,0:T(8,128)}, u32[]{:S(2)}) copy-start(f32[384,512]{1,0:T(8,128)} %fusion.7) | copy-start | bytes 2359300
  329.1 7.9 %slice-start.4 = ((s8[8388608]{0:T(1024)(128)(4,1)}), s8[4194304]{0:T(1024)(128)(4,1)S(1)}, s32[]{:S(2)}) async-start(s8[8388608]{0:T(1024)(128)(4,1)} %bitcast.120), calls=%async_computation.8 | async-start | bytes 8388608
  333.1 3.9 %slice-start.5 = ((s8[8388608]{0:T(1024)(128)(4,1)}), s8[4194304]{0:T(1024)(128)(4,1)S(1)}, s32[]{:S(2)}) async-start(s8[8388608]{0:T(1024)(128)(4,1)} %bitcast.120), calls=%async_computation.9 | async-start | bytes 8388608
  333.1 3.9 %copy-start.7 = (f32[384,512]{1,0:T(8,128)S(1)}, f32[384,512]{1,0:T(8,128)}, u32[]{:S(2)}) copy-start(f32[384,512]{1,0:T(8,128)} %fusion.11) | copy-start | bytes 2359300
  337.0 3.8 %copy-start.5 = (f32[384,512]{1,0:T(8,128)S(1)}, f32[384,512]{1,0:T(8,128)}, u32[]{:S(2)}) copy-start(f32[384,512]{1,0:T(8,128)} %fusion.8) | copy-start | bytes 2359300
Sparse Core Ops, SparseCore 0:
  9.7 77.0 all-gather.4
  89.0 72.8 all-gather.6
  164.1 72.8 all-gather.8
  239.1 72.8 all-gather.10

commit v2 on v1

--- a/solution.py
+++ b/solution.py
@@ -3,7 +3,7 @@
 from jax import lax
 from jax.sharding import PartitionSpec as P
 
-CHUNKS = 4
+CHUNKS = 1
 
 
 def complex_product(left, right):

time: 361 us -> 233 us (0.65)
  waiting for transfers between devices: 260 us -> 163 us
  matrix products: 68.2 us -> 44.6 us
  local copies, waits for them, and re-layouts: 13.3 us -> 7.36 us
    all_gather x4 -> x1, waiting for transfers between devices: 196 us -> 99.1 us  [body(): gathered = lax.all_gather(piece, 'row', axis=1, tiled=True)]
    dot_general x4 -> x1, matrix products: 22 us -> 11.1 us  [complex_product(): jnp.dot(left[1], right[1], preferred_element_type=jnp.float32)]
    dot_general x4 -> x1, matrix products: 16 us -> 11.1 us  [complex_product(): jnp.dot(left[1], right[0], preferred_element_type=jnp.float32)]
    dot_general x4 -> x1, matrix products: 15.2 us -> 11.2 us  [complex_product(): jnp.dot(left[0], right[0], preferred_element_type=jnp.float32)]
    dot_general x4 -> x1, matrix products: 15 us -> 11.2 us  [complex_product(): jnp.dot(left[0], right[1], preferred_element_type=jnp.float32)]
  transfers between devices with their start and end apart: 5 -> 2, of which waited for: 4 -> 2; matrix products, arithmetic and copies ran while one was open for 11% -> 3% of each run, Pallas kernels for 0% -> 0%
where the time goes in v2:
time: 233 us
  waiting for transfers between devices  163 us (70%)
  matrix products  44.6 us (19%)
  between operations  13.4 us (6%)
  local copies, waits for them, and re-layouts  7.36 us (3%)
  starting transfers between devices  3.06 us (1%)
    all_gather x1, waiting for transfers between devices, body(): gathered = lax.all_gather(piece, 'row', axis=1, tiled=True)  99.1 us
    ppermute x1, waiting for transfers between devices, body(): block = lax.ppermute(coeffs, 'band', perm)  62.9 us
    dot_general x1, matrix products, complex_product(): jnp.dot(left[0], right[0], preferred_element_type=jnp.float32)  11.2 us
    dot_general x1, matrix products, complex_product(): jnp.dot(left[0], right[1], preferred_element_type=jnp.float32)  11.2 us
    dot_general x1, matrix products, complex_product(): jnp.dot(left[1], right[0], preferred_element_type=jnp.float32)  11.1 us
    dot_general x1, matrix products, complex_product(): jnp.dot(left[1], right[1], preferred_element_type=jnp.float32)  11.1 us
  transfers between devices with their start and end apart: 2, of which 2 were waited for; matrix products, arithmetic and copies ran while one was open for 3% of the time, Pallas kernels for 0%

profile of v2, /device:TPU:0, one launch (start us, length us, event | category | flops | bytes accessed | tf_op | source)
XLA Modules:
  0.0 233.1 jit_solution(5800816912301786150)
XLA Ops:
  6.5 0.0 all-gather.2.cloned.1.call-start
  6.5 0.7 all-gather.2.cloned.1.call-update
  7.3 3.1 %collective-permute-start = (bf16[2,384,2048]{2,1,0:T(8,128)(2,1)}, bf16[2,384,2048]{2,1,0:T(8,128)(2,1)S(1)}, u32[]{:S(2)}, u32[]{:S(2)}) collective-permute-start(bf16[2,384,2048]{2,1,0:T(8,128)(2,1)} %param.2), channel_id=1, source_target_pairs={{0,16},{16,0},{1,17},{17,1},{2,18},{18,2},{3,19},{19,3},{4,20},{20... | collective-permute-start | bytes 9437192 | tf_op jit(solution)/shard_map/ppermute | solution.py:29
  10.3 0.0 copy-start
  10.3 3.4 %broadcast_in_dim.3 = bf16[2,384,4096]{2,1,0:T(8,128)(2,1)} broadcast(bf16[]{:T(256)} %constant.7.clone.1), dimensions={} | broadcast | bytes 6291458 | tf_op jit(solution)/shard_map/broadcast_in_dim | solution.py:25
  13.7 0.0 copy-done
  13.7 2.0 constant_dynamic-update-slice_fusion.1
  15.7 62.9 %collective-permute-done = bf16[2,384,2048]{2,1,0:T(8,128)(2,1)S(1)} collective-permute-done((bf16[2,384,2048]{2,1,0:T(8,128)(2,1)}, bf16[2,384,2048]{2,1,0:T(8,128)(2,1)S(1)}, u32[]{:S(2)}, u32[]{:S(2)}) %collective-permute-start) | collective-permute-done | bytes 3145760 | tf_op jit(solution)/shard_map/ppermute | solution.py:29
  78.6 1.9 constant_dynamic-update-slice_fusion
  80.6 99.1 %all-gather.2.cloned.1.call-done = bf16[2,4096,2048]{2,1,0:T(8,128)(2,1)} async-done(((bf16[2,256,2048]{2,1,0:T(8,128)(2,1)}), bf16[2,4096,2048]{2,1,0:T(8,128)(2,1)}) %all-gather.2.cloned.1.call-update) | async-done | bytes 33554448 | tf_op jit(solution)/shard_map/all_gather | solution.py:36
  179.7 11.1 %fusion.3 = f32[384,2048]{1,0:T(8,128)S(1)} fusion(bf16[2,4096,2048]{2,1,0:T(8,128)(2,1)} %all-gather.2.cloned.1.call-done, bf16[2,384,4096]{2,1,0:T(8,128)(2,1)} %constant_dynamic-update-slice_fusion), kind=kOutput, calls=%fused_computation.5 | convolution fusion | flops 6442450944 | bytes 23068672 | tf_op jit(solution)/shard_map/dot_general | solution.py:10
  190.8 11.1 %fusion = f32[384,2048]{1,0:T(8,128)S(1)} fusion(bf16[2,4096,2048]{2,1,0:T(8,128)(2,1)} %all-gather.2.cloned.1.call-done, bf16[2,384,4096]{2,1,0:T(8,128)(2,1)} %constant_dynamic-update-slice_fusion), kind=kOutput, calls=%fused_computation.2 | convolution fusion | flops 6442450944 | bytes 23068672 | tf_op jit(solution)/shard_map/dot_general | solution.py:13
  201.9 11.2 %fusion.4 = bf16[1,384,2048]{2,1,0:T(8,128)(2,1)S(1)} fusion(f32[384,2048]{1,0:T(8,128)S(1)} %fusion.3, bf16[2,4096,2048]{2,1,0:T(8,128)(2,1)} %all-gather.2.cloned.1.call-done, bf16[2,384,4096]{2,1,0:T(8,128)(2,1)} %constant_dynamic-update-slice_fusion), kind=kOutput, calls=%fused_computation.11 | convolution fusion | flops 6444023808 | bytes 24641536 | tf_op jit(solution)/shard_map/dot_general | solution.py:10
  213.1 11.2 %fusion.5 = bf16[1,384,2048]{2,1,0:T(8,128)(2,1)S(1)} fusion(f32[384,2048]{1,0:T(8,128)S(1)} %fusion, bf16[2,4096,2048]{2,1,0:T(8,128)(2,1)} %all-gather.2.cloned.1.call-done, bf16[2,384,4096]{2,1,0:T(8,128)(2,1)} %constant_dynamic-update-slice_fusion), kind=kOutput, calls=%fused_computation.12 | convolution fusion | flops 6444023808 | bytes 24641536 | tf_op jit(solution)/shard_map/dot_general | solution.py:13
  224.3 1.9 pad_maximum_fusion
Async XLA Ops:
  6.5 173.1 %all-gather.2.cloned.1.call-start = ((), (), s32[]{:S(2)}) async-start(), calls=%async_computation | async-start | bytes 35651584 | tf_op jit(solution)/shard_map/all_gather | solution.py:36
  7.3 71.4 %collective-permute-start = (bf16[2,384,2048]{2,1,0:T(8,128)(2,1)}, bf16[2,384,2048]{2,1,0:T(8,128)(2,1)S(1)}, u32[]{:S(2)}, u32[]{:S(2)}) collective-permute-start(bf16[2,384,2048]{2,1,0:T(8,128)(2,1)} %param.2), channel_id=1, source_target_pairs={{0,16},{16,0},{1,17},{17,1},{2,18},{18,2},{3,19},{19,3},{4,20},{20... | collective-permute-start | bytes 9437192 | tf_op jit(solution)/shard_map/ppermute | solution.py:29
  10.3 3.4 %copy-start = (bf16[2,384,2048]{2,1,0:T(8,128)(2,1)S(1)}, bf16[2,384,2048]{2,1,0:T(8,128)(2,1)}, u32[]{:S(2)}) copy-start(bf16[2,384,2048]{2,1,0:T(8,128)(2,1)} %param.2) | copy-start | bytes 9437188
Sparse Core Ops, SparseCore 0:
  8.9 170.7 all-gather.1

commit v3 on v0

v3 whole, which is shorter than its diff:
```python
import functools

import jax
import jax.numpy as jnp
from jax import lax
from jax.experimental import pallas as pl
from jax.experimental.pallas import tpu as pltpu
from jax.sharding import PartitionSpec as P

MESH = pl.DeviceIdType.MESH
CORES = 2
SUBS = 2


def kernel(chips, bands, tile, coeffs_ref, rotation_ref, out_ref, held, whole, total,
           ring_send, ring_recv, pair_send, pair_recv, band_send, band_recv, own_sem):
    band = lax.axis_index("band")
    row = lax.axis_index("row")
    depth = rotation_ref.shape[1]
    columns = rotation_ref.shape[2]
    width = coeffs_ref.shape[2]
    sub = depth // SUBS
    half = chips // 2

    chip = row // CORES
    core = row % CORES
    line = chip // 2
    side = chip % 2
    place = line + side * (chips - 1 - 2 * line)

    def chip_at(position):
        back = position // half
        return (1 - back) * 2 * position + back * (2 * (chips - 1 - position) + 1)

    ahead = chip_at((place + 1) % chips) * CORES + core
    behind = chip_at((place + chips - 1) % chips) * CORES + core
    sibling = chip * CORES + (1 - core)
    partners = [(band + step) % bands for step in range(1, bands)]

    barrier = pltpu.get_barrier_semaphore()
    for other in (ahead, behind, sibling):
        pl.semaphore_signal(barrier, inc=1, device_id={"row": other}, device_id_type=MESH)
    for other in partners:
        pl.semaphore_signal(barrier, inc=1, device_id={"band": other}, device_id_type=MESH)
    pl.semaphore_wait(barrier, 3 + len(partners))

    def mine(part, step, piece):
        start = pl.multiple_of(core * depth + piece * sub, sub)
        return held.at[part, step, pl.ds(start, sub)]

    def source(part, step, piece):
        if step == 0:
            return rotation_ref.at[part, pl.ds(piece * sub, sub)]
        return mine(part, step, piece)

    def hop(part, step, piece):
        return pltpu.make_async_remote_copy(
            src_ref=source(part, step, piece),
            dst_ref=mine(part, step + 1, piece),
            send_sem=ring_send.at[part, step, piece],
            recv_sem=ring_recv.at[part, step, piece],
            device_id={"row": (ahead, behind)[part]},
            device_id_type=MESH,
        )

    def share(part, step, piece):
        return pltpu.make_async_remote_copy(
            src_ref=source(part, step, piece),
            dst_ref=mine(part, step, piece),
            send_sem=pair_send.at[part, step, piece],
            recv_sem=pair_recv.at[part, step, piece],
            device_id={"row": sibling},
            device_id_type=MESH,
        )

    pieces = [(part, piece) for piece in range(SUBS) for part in range(2)]
    for part, piece in pieces:
        hop(part, 0, piece).start()
    spread = [
        pltpu.make_async_remote_copy(
            src_ref=coeffs_ref,
            dst_ref=whole.at[band],
            send_sem=band_send.at[i],
            recv_sem=band_recv.at[i],
            device_id={"band": other},
            device_id_type=MESH,
        )
        for i, other in enumerate(partners)
    ]
    for copy in spread:
        copy.start()
    for part, piece in pieces:
        share(part, 0, piece).start()
    own = [pltpu.make_async_copy(coeffs_ref, whole.at[band], own_sem.at[0])]
    for part in range(2):
        start = pl.multiple_of(core * depth, depth)
        own.append(
            pltpu.make_async_copy(rotation_ref.at[part], held.at[part, 0, pl.ds(start, depth)], own_sem.at[1 + part])
        )
    for copy in own:
        copy.start()
    for copy in own:
        copy.wait()

    def multiply(step):
        for part, piece in pieces:
            share(part, step, piece).wait_recv()
        spans = []
        for origin in ((place + chips - step) % chips, (place + step) % chips):
            first = chip_at(origin) * (CORES * depth)
            spans.append((first // width, pl.multiple_of(first % width, CORES * depth)))

        def left(part, span):
            return whole[span[0], part, :, pl.ds(span[1], CORES * depth)]

        @pl.loop(0, columns // tile)
        def _(i):
            cut = pl.ds(pl.multiple_of(i * tile, tile), tile)
            real = held[0, step, :, cut]
            imag = held[1, step, :, cut]
            dot = functools.partial(jnp.dot, preferred_element_type=jnp.float32)
            real_term = dot(left(0, spans[0]), real) - dot(left(1, spans[1]), imag)
            if step > 0:
                real_term += total[0, :, cut]
            imag_term = dot(left(1, spans[0]), real) + dot(left(0, spans[1]), imag)
            if step > 0:
                imag_term += total[1, :, cut]
            if step < chips - 1:
                total[0, :, cut] = real_term
                total[1, :, cut] = imag_term
            else:
                out_ref[0, :, cut] = real_term.astype(out_ref.dtype)
                out_ref[1, :, cut] = imag_term.astype(out_ref.dtype)

    events = (chips - 1) * SUBS
    event = 0
    for step in range(1, chips):
        for piece in range(SUBS):
            for part in range(2):
                hop(part, step - 1, piece).wait_recv()
                if step < chips - 1:
                    hop(part, step, piece).start()
                share(part, step, piece).start()
            ready = event - (events - chips)
            if ready == 0:
                for copy in spread:
                    copy.wait_recv()
            if ready >= 0:
                multiply(ready)
            event += 1

    for copy in spread:
        copy.wait_send()
    for step in range(chips):
        for part, piece in pieces:
            if step < chips - 1:
                hop(part, step, piece).wait_send()
            share(part, step, piece).wait_send()


def solution(mesh):
    bands, rows = mesh.shape["band"], mesh.shape["row"]
    chips = rows // CORES

    def body(coeffs, rotation):
        depth, columns = rotation.shape[1:]
        tile = min(256, columns)
        return pl.pallas_call(
            functools.partial(kernel, chips, bands, tile),
            out_shape=jax.ShapeDtypeStruct(coeffs.shape, jnp.bfloat16),
            in_specs=[pl.BlockSpec(memory_space=pl.ANY)] * 2,
            out_specs=pl.BlockSpec(memory_space=pltpu.VMEM),
            scratch_shapes=[
                pltpu.VMEM((2, chips, CORES * depth, columns), jnp.bfloat16),
                pltpu.VMEM((bands,) + coeffs.shape, jnp.bfloat16),
                pltpu.VMEM(coeffs.shape, jnp.float32),
                pltpu.SemaphoreType.DMA((2, chips - 1, SUBS)),
                pltpu.SemaphoreType.DMA((2, chips - 1, SUBS)),
                pltpu.SemaphoreType.DMA((2, chips, SUBS)),
                pltpu.SemaphoreType.DMA((2, chips, SUBS)),
                pltpu.SemaphoreType.DMA((bands - 1,)),
                pltpu.SemaphoreType.DMA((bands - 1,)),
                pltpu.SemaphoreType.DMA((3,)),
            ],
            compiler_params=pltpu.CompilerParams(
                collective_id=0, has_side_effects=True, vmem_limit_bytes=62 * 1024 * 1024
            ),
        )(coeffs, rotation)

    in_specs = (P(None, "row", "band"), P(None, "row", "band"))
    out_specs = P(None, "row", "band")
    return jax.shard_map(body, mesh=mesh, in_specs=in_specs, out_specs=out_specs, check_vma=False)
```

time: 313 us -> 176 us (0.56)
  waiting for transfers between devices: 255 us -> 0 us
  Pallas kernels: 0 us -> 171 us
  matrix products: 42.3 us -> 0 us
  between operations: 13.4 us -> 0.01 us
  local copies, waits for them, and re-layouts: 0.01 us -> 3.97 us
    all_gather x2 -> x0, waiting for transfers between devices: 254 us -> none  [the longest x1 170 us: body(): lax.all_gather(rotation, 'row', axis=1, tiled=True)]
    pallas_call x0 -> x1, Pallas kernels: none -> 171 us  [body(): pl.pallas_call(functools.partial(kernel, chips, bands, tile), out_shape=j...]
    dot_general x4 -> x0, matrix products: 42.3 us -> none  [the longest x1 11.3 us: complex_product(): jnp.dot(left[1], right[0], preferred_element_type=jnp.float32)]
    unnamed x2 -> x1, local copies, waits for them, and re-layouts: 0.01 us -> 3.97 us
  transfers between devices with their start and end apart: 2 -> 0, of which waited for: 2 -> 0; matrix products, arithmetic and copies ran while one was open for 0% -> 0% of each run, Pallas kernels for 0% -> 0%
where the time goes in v3:
time: 176 us; the launch traced here: 175 us
  Pallas kernels  171 us (97%)
  local copies, waits for them, and re-layouts  3.97 us (2%)
    pallas_call x1, Pallas kernels, body(): pl.pallas_call(functools.partial(kernel, chips, bands, tile), out_shape=j...  171 us
    unnamed x1, local copies, waits for them, and re-layouts  3.97 us

profile of v3, /device:TPU:0, one launch (start us, length us, event | category | flops | bytes accessed | tf_op | source)
XLA Modules:
  0.0 175.2 jit_solution(18273630059820849705)
XLA Ops:
  0.0 171.2 %shard_map.28 = bf16[2,384,2048]{2,1,0:T(8,128)(2,1)} custom-call(bf16[2,384,2048]{2,1,0:T(8,128)(2,1)} %coeffs_ref.1, bf16[2,256,2048]{2,1,0:T(8,128)(2,1)} %rotation_ref.1), custom_call_target="tpu_custom_call" | custom-call | tf_op jit(solution)/shard_map/pallas_call | solution.py:168
  171.2 4.0 %copy.4 = bf16[2,384,2048]{2,1,0:T(8,128)(2,1)} copy(bf16[2,384,2048]{2,1,0:T(8,128)(2,1)} %shard_map.28) | data formatting | bytes 6291456

commit v4 on v3

--- a/solution.py
+++ b/solution.py
@@ -9,17 +9,16 @@
 
 MESH = pl.DeviceIdType.MESH
 CORES = 2
-SUBS = 2
+PIECE_BYTES = 256 * 1024
 
 
-def kernel(chips, bands, tile, coeffs_ref, rotation_ref, out_ref, held, whole, total,
+def kernel(chips, bands, cuts, tile, coeffs_ref, rotation_ref, out_ref, held, whole, total,
            ring_send, ring_recv, pair_send, pair_recv, band_send, band_recv, own_sem):
     band = lax.axis_index("band")
     row = lax.axis_index("row")
     depth = rotation_ref.shape[1]
-    columns = rotation_ref.shape[2]
+    columns = rotation_ref.shape[2] // cuts
     width = coeffs_ref.shape[2]
-    sub = depth // SUBS
     half = chips // 2
 
     chip = row // CORES
@@ -45,12 +44,11 @@
     pl.semaphore_wait(barrier, 3 + len(partners))
 
     def mine(part, step, piece):
-        start = pl.multiple_of(core * depth + piece * sub, sub)
-        return held.at[part, step, pl.ds(start, sub)]
+        return held.at[part, step, piece, pl.ds(pl.multiple_of(core * depth, depth), depth)]
 
     def source(part, step, piece):
         if step == 0:
-            return rotation_ref.at[part, pl.ds(piece * sub, sub)]
+            return rotation_ref.at[part, :, pl.ds(piece * columns, columns)]
         return mine(part, step, piece)
 
     def hop(part, step, piece):
@@ -73,7 +71,7 @@
             device_id_type=MESH,
         )
 
-    pieces = [(part, piece) for piece in range(SUBS) for part in range(2)]
+    pieces = [(part, piece) for piece in range(cuts) for part in range(2)]
     for part, piece in pieces:
         hop(part, 0, piece).start()
     spread = [
@@ -92,18 +90,15 @@
     for part, piece in pieces:
         share(part, 0, piece).start()
     own = [pltpu.make_async_copy(coeffs_ref, whole.at[band], own_sem.at[0])]
-    for part in range(2):
-        start = pl.multiple_of(core * depth, depth)
-        own.append(
-            pltpu.make_async_copy(rotation_ref.at[part], held.at[part, 0, pl.ds(start, depth)], own_sem.at[1 + part])
-        )
+    for i, (part, piece) in enumerate(pieces):
+        own.append(pltpu.make_async_copy(source(part, 0, piece), mine(part, 0, piece), own_sem.at[1 + i]))
     for copy in own:
         copy.start()
     for copy in own:
         copy.wait()
 
-    def multiply(step):
-        for part, piece in pieces:
+    def multiply(step, piece):
+        for part in range(2):
             share(part, step, piece).wait_recv()
         spans = []
         for origin in ((place + chips - step) % chips, (place + step) % chips):
@@ -116,38 +111,44 @@
         @pl.loop(0, columns // tile)
         def _(i):
             cut = pl.ds(pl.multiple_of(i * tile, tile), tile)
-            real = held[0, step, :, cut]
-            imag = held[1, step, :, cut]
+            out = pl.ds(pl.multiple_of(piece * columns + i * tile, tile), tile)
+            real = held[0, step, piece, :, cut]
+            imag = held[1, step, piece, :, cut]
             dot = functools.partial(jnp.dot, preferred_element_type=jnp.float32)
             real_term = dot(left(0, spans[0]), real) - dot(left(1, spans[1]), imag)
             if step > 0:
-                real_term += total[0, :, cut]
+                real_term += total[0, :, out]
             imag_term = dot(left(1, spans[0]), real) + dot(left(0, spans[1]), imag)
             if step > 0:
-                imag_term += total[1, :, cut]
+                imag_term += total[1, :, out]
             if step < chips - 1:
-                total[0, :, cut] = real_term
-                total[1, :, cut] = imag_term
+                total[0, :, out] = real_term
+                total[1, :, out] = imag_term
             else:
-                out_ref[0, :, cut] = real_term.astype(out_ref.dtype)
-                out_ref[1, :, cut] = imag_term.astype(out_ref.dtype)
+                out_ref[0, :, out] = real_term.astype(out_ref.dtype)
+                out_ref[1, :, out] = imag_term.astype(out_ref.dtype)
 
-    events = (chips - 1) * SUBS
-    event = 0
-    for step in range(1, chips):
-        for piece in range(SUBS):
-            for part in range(2):
-                hop(part, step - 1, piece).wait_recv()
-                if step < chips - 1:
-                    hop(part, step, piece).start()
-                share(part, step, piece).start()
-            ready = event - (events - chips)
-            if ready == 0:
-                for copy in spread:
-                    copy.wait_recv()
-            if ready >= 0:
-                multiply(ready)
-            event += 1
+    units = [(step, piece) for step in range(chips) for piece in range(cuts)]
+    events = (chips - 1) * cuts
+    begin = events // 2
+    done = 0
+    for event in range(events):
+        step, piece = 1 + event // cuts, event % cuts
+        for part in range(2):
+            hop(part, step - 1, piece).wait_recv()
+            if step < chips - 1:
+                hop(part, step, piece).start()
+            share(part, step, piece).start()
+        if event == begin:
+            for copy in spread:
+                copy.wait_recv()
+        if event >= begin:
+            goal = min(event + cuts, 3 * (event - begin + 1))
+            for unit in units[done:goal]:
+                multiply(*unit)
+            done = max(done, goal)
+    for unit in units[done:]:
+        multiply(*unit)
 
     for copy in spread:
         copy.wait_send()
@@ -164,26 +165,27 @@
 
     def body(coeffs, rotation):
         depth, columns = rotation.shape[1:]
-        tile = min(256, columns)
+        cuts = max(1, min(4, depth * columns * 2 // PIECE_BYTES))
+        tile = min(256, columns // cuts)
         return pl.pallas_call(
-            functools.partial(kernel, chips, bands, tile),
+            functools.partial(kernel, chips, bands, cuts, tile),
             out_shape=jax.ShapeDtypeStruct(coeffs.shape, jnp.bfloat16),
             in_specs=[pl.BlockSpec(memory_space=pl.ANY)] * 2,
             out_specs=pl.BlockSpec(memory_space=pltpu.VMEM),
             scratch_shapes=[
-                pltpu.VMEM((2, chips, CORES * depth, columns), jnp.bfloat16),
+                pltpu.VMEM((2, chips, cuts, CORES * depth, columns // cuts), jnp.bfloat16),
                 pltpu.VMEM((bands,) + coeffs.shape, jnp.bfloat16),
                 pltpu.VMEM(coeffs.shape, jnp.float32),
-                pltpu.SemaphoreType.DMA((2, chips - 1, SUBS)),
-                pltpu.SemaphoreType.DMA((2, chips - 1, SUBS)),
-                pltpu.SemaphoreType.DMA((2, chips, SUBS)),
-                pltpu.SemaphoreType.DMA((2, chips, SUBS)),
+                pltpu.SemaphoreType.DMA((2, chips - 1, cuts)),
+                pltpu.SemaphoreType.DMA((2, chips - 1, cuts)),
+                pltpu.SemaphoreType.DMA((2, chips, cuts)),
+                pltpu.SemaphoreType.DMA((2, chips, cuts)),
                 pltpu.SemaphoreType.DMA((bands - 1,)),
                 pltpu.SemaphoreType.DMA((bands - 1,)),
-                pltpu.SemaphoreType.DMA((3,)),
+                pltpu.SemaphoreType.DMA((1 + 2 * cuts,)),
             ],
             compiler_params=pltpu.CompilerParams(
-                collective_id=0, has_side_effects=True, vmem_limit_bytes=62 * 1024 * 1024
+                collective_id=0, has_side_effects=True, vmem_limit_bytes=54 * 1024 * 1024
             ),
         )(coeffs, rotation)
 

time: 176 us -> 173 us (0.983)
  Pallas kernels: 171 us -> 169 us
    pallas_call x1, Pallas kernels: 171 us -> 169 us  [body(): pl.pallas_call(functools.partial(kernel, chips, bands, cuts, tile), out_s...]
where the time goes in v4:
time: 173 us
  Pallas kernels  169 us (98%)
  local copies, waits for them, and re-layouts  3.97 us (2%)
    pallas_call x1, Pallas kernels, body(): pl.pallas_call(functools.partial(kernel, chips, bands, cuts, tile), out_s...  169 us
    unnamed x1, local copies, waits for them, and re-layouts  3.97 us

profile of v4, /device:TPU:0, one launch (start us, length us, event | category | flops | bytes accessed | tf_op | source)
XLA Modules:
  0.0 173.0 jit_solution(2003733169788289299)
XLA Ops:
  0.0 169.0 %shard_map.28 = bf16[2,384,2048]{2,1,0:T(8,128)(2,1)} custom-call(bf16[2,384,2048]{2,1,0:T(8,128)(2,1)} %coeffs_ref.1, bf16[2,256,2048]{2,1,0:T(8,128)(2,1)} %rotation_ref.1), custom_call_target="tpu_custom_call" | custom-call | tf_op jit(solution)/shard_map/pallas_call | solution.py:170
  169.0 4.0 %copy.4 = bf16[2,384,2048]{2,1,0:T(8,128)(2,1)} copy(bf16[2,384,2048]{2,1,0:T(8,128)(2,1)} %shard_map.28) | data formatting | bytes 6291456

commit v5 on v4

--- a/solution.py
+++ b/solution.py
@@ -169,7 +169,7 @@
         tile = min(256, columns // cuts)
         return pl.pallas_call(
             functools.partial(kernel, chips, bands, cuts, tile),
-            out_shape=jax.ShapeDtypeStruct(coeffs.shape, jnp.bfloat16),
+            out_shape=pltpu.VMEM(coeffs.shape, jnp.bfloat16),
             in_specs=[pl.BlockSpec(memory_space=pl.ANY)] * 2,
             out_specs=pl.BlockSpec(memory_space=pltpu.VMEM),
             scratch_shapes=[

time: 173 us -> 169 us (0.977)
  local copies, waits for them, and re-layouts: 3.97 us -> 1.67 us
  Pallas kernels: 169 us -> 167 us
    unnamed x1, local copies, waits for them, and re-layouts: 3.97 us -> 1.67 us
where the time goes in v5:
time: 169 us
  Pallas kernels  167 us (99%)
    pallas_call x1, Pallas kernels, body(): pl.pallas_call(functools.partial(kernel, chips, bands, cuts, tile), out_s...  167 us

profile of v5, /device:TPU:0, one launch (start us, length us, event | category | flops | bytes accessed | tf_op | source)
XLA Modules:
  0.0 169.0 jit_solution(13264953546038983685)
XLA Ops:
  0.0 167.3 %shard_map.28 = bf16[2,384,2048]{2,1,0:T(8,128)(2,1)S(1)} custom-call(bf16[2,384,2048]{2,1,0:T(8,128)(2,1)} %coeffs_ref.1, bf16[2,256,2048]{2,1,0:T(8,128)(2,1)} %rotation_ref.1), custom_call_target="tpu_custom_call" | custom-call | tf_op jit(solution)/shard_map/pallas_call | solution.py:170
  167.3 1.7 copy.4
